TPU v7x, 32 devices: a whole 2x2x4 slice. The times are simulated.
32 devices in a mesh: groups: 2 (over y), seq: 4 (over z), fsdp: 4 (over x, core).
Axes of the slice: x: 2, y: 2, z: 4, core: 2. Of those that a mesh axis runs over, the one named last changes fastest.
Arguments:
- tokens: bfloat16 [1024, 1024], P(('groups', 'seq')), parts along dimension 0, may hold values from -16 to 16
- qkv_weight: bfloat16 [1024, 1536], P('seq', 'fsdp'), may hold values from -0.125 to 0.125
- covisible: int32 [8, 4], P('groups'), parts along dimension 0, may hold values 0 or 1
- block_drive: int32 [8], P('groups'), parts along dimension 0, may hold values from 0 to 2
- grad_out: bfloat16 [1024, 512], P(('groups', 'seq'), 'fsdp'), parts along dimension 0, may hold values from -6 to 6
Outputs:
- attention: bfloat16 [1024, 512], P(('groups', 'seq'), 'fsdp'), parts along dimension 0
- grad_input: bfloat16 [1024, 1024], P(('groups', 'seq'), 'fsdp'), parts along dimension 0
- grad_weight: float32 [2048, 1536], P(('groups', 'seq'), 'fsdp'), parts along dimension 0
There are 2 independent parts, one for each index of `groups`. A program takes and returns all parts, laid end to end along the dimension named above; an argument that names none is the same for every part. Nothing has to cross between parts.
All inputs are finite; a program needn't handle non-finite values.
Results may differ from a plain program's by a relative error of at most 0.018.
The roundings to bfloat16 on the way count: a program that leaves them out, or rounds other values in their place, can miss the bound.
Values may be sent and summed in bfloat16 or wider, within the bound.
No kernel may reach another device: no remote copies, remote signals or barrier semaphores. Data moves between devices by JAX's collectives and lax.ppermute only.
A program may use at most 64 MiB of HBM per device.

v0:
```python
import jax
import jax.numpy as jnp
from jax import lax
from jax.sharding import PartitionSpec as P

HD = 64
BLOCK = 128
MASKED_SCORE = -1e30


def query_visible(covisible, block_drive, first_block, block_count):
    own_rows = lax.dynamic_slice_in_dim(covisible, first_block, block_count, 0)
    own_drive = lax.dynamic_slice_in_dim(block_drive, first_block, block_count, 0)
    joined = jnp.logical_or(own_rows == 1, own_drive[:, None] == block_drive[None, :])
    return joined.astype(jnp.float32)


def key_visible(covisible, block_drive, first_block, block_count):
    own_columns = lax.dynamic_slice_in_dim(covisible, first_block, block_count, 1)
    own_drive = lax.dynamic_slice_in_dim(block_drive, first_block, block_count, 0)
    joined = jnp.logical_or(own_columns == 1, block_drive[:, None] == own_drive[None, :])
    return joined.astype(jnp.float32)


def block_onehot(length, block_total):
    member = lax.iota(jnp.int32, length) // BLOCK
    return (member[:, None] == lax.iota(jnp.int32, block_total)[None, :]).astype(jnp.float32)


def per_device(tokens, qkv_weight, covisible, block_drive, grad_out):
    local_rows = tokens.shape[0]
    seq_count = lax.axis_size("seq")
    seq_index = lax.axis_index("seq")
    out_width = qkv_weight.shape[1]
    local_heads = out_width // (3 * HD)
    block_count = local_rows // BLOCK
    block_total = covisible.shape[0]
    first_block = seq_index * block_count
    scaling = HD ** (-0.5)
    rows_visible = query_visible(covisible, block_drive, first_block, block_count)
    columns_visible = key_visible(covisible, block_drive, first_block, block_count)
    inputs = tokens
    projected = jnp.dot(
        inputs,
        lax.all_gather(qkv_weight, "seq", axis=0, tiled=True),
        preferred_element_type=jnp.float32,
    )
    projected = projected.astype(jnp.bfloat16).reshape(local_rows, local_heads, 3, HD)
    queries = projected[:, :, 0, :]
    local_keys = projected[:, :, 1, :]
    local_values = projected[:, :, 2, :]
    key_value = projected[:, :, 1:, :].reshape(local_rows, local_heads * 2 * HD)

    def local_visible(length):
        onehot = block_onehot(length, block_total)
        return (jnp.repeat(jnp.dot(rows_visible, onehot.T), BLOCK, axis=0) > 0.5)[None]

    panel = lax.all_gather(key_value, "seq", axis=0, tiled=True)
    running_max = jnp.full((local_heads, local_rows), MASKED_SCORE, jnp.float32)
    length = panel.shape[0]
    visible = local_visible(length)
    split_panel = panel.reshape(length, local_heads, 2, HD)
    scores = (
        jnp.einsum(
            "qhd,khd->hqk", queries, split_panel[:, :, 0, :], preferred_element_type=jnp.float32
        )
        * scaling
    )
    new_max = jnp.maximum(running_max, jnp.where(visible, scores, MASKED_SCORE).max(axis=2))
    shifted = jnp.exp(jnp.where(visible, scores - new_max[:, :, None], MASKED_SCORE))
    running_sum = shifted.sum(axis=2)
    wide_values = split_panel[:, :, 1, :].astype(jnp.float32)
    weighted = jnp.einsum(
        "hqk,khd->hqd",
        shifted,
        wide_values,
        precision=lax.Precision.HIGHEST,
        preferred_element_type=jnp.float32,
    )
    running_max, running_sum, weighted = (new_max, running_sum, weighted)
    attention_heads = (weighted / running_sum[:, :, None]).astype(jnp.bfloat16)
    attention = jnp.transpose(attention_heads, (1, 0, 2)).reshape(local_rows, local_heads * HD)
    log_total = running_max + jnp.log(running_sum)
    grad_heads = grad_out.reshape(local_rows, local_heads, HD)
    grad_dot_rows = jnp.sum(
        grad_heads.astype(jnp.float32)
        * attention.reshape(local_rows, local_heads, HD).astype(jnp.float32),
        axis=2,
    )
    grad_dot = jnp.transpose(grad_dot_rows)
    log_total_rows = jnp.transpose(log_total)
    all_log_total, all_grad_dot = (
        lax.all_gather(log_total_rows, "seq", axis=0, tiled=True),
        lax.all_gather(grad_dot_rows, "seq", axis=0, tiled=True),
    )
    query_rows = queries.reshape(local_rows, local_heads * HD)
    far_queries = lax.all_gather(query_rows, "seq", axis=0, tiled=True)
    far_grads = lax.all_gather(grad_out, "seq", axis=0, tiled=True)
    length = far_queries.shape[0]
    onehot = block_onehot(length, block_total)
    visible = (jnp.repeat(jnp.dot(onehot, columns_visible), BLOCK, axis=1) > 0.5)[None]
    far_heads = far_queries.reshape(length, local_heads, HD)
    far_grad_heads = far_grads.reshape(length, local_heads, HD)
    far_log_total = jnp.transpose(all_log_total)
    far_grad_dot = jnp.transpose(all_grad_dot)
    scores = (
        jnp.einsum("qhd,khd->hqk", far_heads, local_keys, preferred_element_type=jnp.float32)
        * scaling
    )
    probabilities = jnp.exp(jnp.where(visible, scores - far_log_total[:, :, None], MASKED_SCORE))
    grad_prob = jnp.einsum(
        "qhd,khd->hqk", far_grad_heads, local_values, preferred_element_type=jnp.float32
    )
    grad_score = (probabilities * (grad_prob - far_grad_dot[:, :, None]) * scaling).astype(
        jnp.bfloat16
    )
    grad_keys = jnp.einsum(
        "hqk,qhd->khd", grad_score, far_heads, preferred_element_type=jnp.float32
    )
    grad_values = jnp.einsum(
        "hqk,qhd->khd",
        probabilities.astype(jnp.bfloat16),
        far_grad_heads,
        preferred_element_type=jnp.float32,
    )
    grad_keys, grad_values = (grad_keys, grad_values)
    panel = lax.all_gather(key_value, "seq", axis=0, tiled=True)
    length = panel.shape[0]
    visible = local_visible(length)
    split_panel = panel.reshape(length, local_heads, 2, HD)
    panel_keys = split_panel[:, :, 0, :]
    scores = (
        jnp.einsum("qhd,khd->hqk", queries, panel_keys, preferred_element_type=jnp.float32)
        * scaling
    )
    probabilities = jnp.exp(jnp.where(visible, scores - log_total[:, :, None], MASKED_SCORE))
    grad_prob = jnp.einsum(
        "qhd,khd->hqk", grad_heads, split_panel[:, :, 1, :], preferred_element_type=jnp.float32
    )
    grad_score = (probabilities * (grad_prob - grad_dot[:, :, None]) * scaling).astype(jnp.bfloat16)
    grad_queries = jnp.einsum(
        "hqk,khd->qhd", grad_score, panel_keys, preferred_element_type=jnp.float32
    )
    grad_qkv = (
        jnp.stack([grad_queries, grad_keys, grad_values], axis=2)
        .astype(jnp.bfloat16)
        .reshape(local_rows, out_width)
    )
    partial_input = lax.dot_general(
        grad_qkv,
        lax.all_gather(qkv_weight, "seq", axis=0, tiled=True),
        (((1,), (1,)), ((), ())),
        preferred_element_type=jnp.float32,
    )
    grad_input = lax.psum_scatter(partial_input, "fsdp", scatter_dimension=1, tiled=True).astype(
        jnp.bfloat16
    )
    token_scale = (local_rows * seq_count) ** (-0.5)
    column_tokens = lax.all_to_all(tokens, "seq", split_axis=1, concat_axis=0, tiled=True)
    inputs = column_tokens
    summed_rows = lax.dot_general(
        inputs,
        lax.all_gather(grad_qkv, "seq", axis=0, tiled=True),
        (((0,), (0,)), ((), ())),
        preferred_element_type=jnp.float32,
    )
    grad_weight = summed_rows * token_scale
    return (attention, grad_input, grad_weight)


def solution(mesh):
    in_specs = (
        P(("groups", "seq"), None),
        P("seq", "fsdp"),
        P("groups", None),
        P("groups"),
        P(("groups", "seq"), "fsdp"),
    )
    out_specs = (
        P(("groups", "seq"), "fsdp"),
        P(("groups", "seq"), "fsdp"),
        P(("groups", "seq"), "fsdp"),
    )
    return jax.shard_map(
        per_device, mesh=mesh, in_specs=in_specs, out_specs=out_specs, check_vma=False
    )
```

profile of v0, /device:TPU:0, one launch (start us, length us, event | category | flops | bytes accessed | tf_op | source)
XLA Modules:
  0.0 121.6 jit_solution(15169649852441177908)
XLA Ops:
  7.2 0.6 copy-done.3
  7.9 0.6 dynamic_slice.11
  8.6 0.9 fusion.35
  9.5 21.6 %all_gather.23 = bf16[1024,384]{1,0:T(8,128)(2,1)S(1)} all-gather(bf16[256,384]{1,0:T(8,128)(2,1)} %param.6), channel_id=1, replica_groups=mesh['groups'=2,'seq'=4,'fsdp'=4] {'seq'}, dimensions={0}, use_global_device_ids=true | all-gather | bytes 983040 | tf_op jit(solution)/shard_map/all_gather | solution.py:45
  31.1 0.3 convolution_convert_fusion
  31.4 0.1 copy.26
  31.6 12.8 %all_gather.24 = bf16[512,256]{0,1:T(8,128)(2,1)S(1)} all-gather(bf16[128,256]{0,1:T(8,128)(2,1)S(1)} %bitcast.145), channel_id=1, replica_groups=mesh['groups'=2,'seq'=4,'fsdp'=4] {'seq'}, dimensions={0}, use_global_device_ids=true | all-gather | bytes 327680 | tf_op jit(solution)/shard_map/all_gather | solution.py:58
  44.4 0.3 select_reduce_fusion
  44.7 0.2 fusion.24
  45.1 0.8 copy-done.1
  45.8 0.1 copy.30
  45.9 13.3 %all_gather.27 = bf16[512,128]{1,0:T(8,128)(2,1)S(1)} all-gather(bf16[128,128]{1,0:T(8,128)(2,1)S(1)} %copy-done.1), channel_id=1, replica_groups=mesh['groups'=2,'seq'=4,'fsdp'=4] {'seq'}, dimensions={0}, use_global_device_ids=true | all-gather | bytes 163840 | tf_op jit(solution)/shard_map/all_gather | solution.py:98
  59.3 8.2 %all_gather.26 = f32[512,2]{0,1:T(2,128)S(1)} all-gather(f32[128,2]{0,1:T(2,128)S(1)} %bitcast_add_fusion), channel_id=1, replica_groups=mesh['groups'=2,'seq'=4,'fsdp'=4] {'seq'}, dimensions={0}, use_global_device_ids=true | all-gather | bytes 5120 | tf_op jit(solution)/shard_map/all_gather | solution.py:93
  67.6 0.9 fusion.34
  68.5 12.3 %all_gather.25 = bf16[512,128]{0,1:T(8,128)(2,1)S(1)} all-gather(bf16[128,128]{0,1:T(8,128)(2,1)S(1)} %bitcast.146), channel_id=1, replica_groups=mesh['groups'=2,'seq'=4,'fsdp'=4] {'seq'}, dimensions={0}, use_global_device_ids=true | all-gather | bytes 163840 | tf_op jit(solution)/shard_map/all_gather | solution.py:97
  80.8 0.6 multiply_reduce_fusion
  81.3 8.0 %all_gather.28 = f32[512,2]{0,1:T(2,128)S(1)} all-gather(f32[128,2]{0,1:T(2,128)S(1)} %get-tuple-element.14), channel_id=1, replica_groups=mesh['groups'=2,'seq'=4,'fsdp'=4] {'seq'}, dimensions={0}, use_global_device_ids=true | all-gather | bytes 5120 | tf_op jit(solution)/shard_map/all_gather | solution.py:94
  89.4 0.1 copy.34
  89.5 0.4 fusion.6
  89.9 0.2 fusion.20
  90.1 0.4 fusion.19
  90.5 0.5 fusion.18
  91.0 1.2 fusion.62
  92.2 0.8 copy.37
  93.0 3.4 %all-to-all-start = ((bf16[128,4,256]{0,2,1:T(8,128)(2,1)}), bf16[128,4,256]{0,2,1:T(8,128)(2,1)S(1)}, u32[]{:S(2)}, u32[]{:S(2)}) async-start(bf16[128,4,256]{0,2,1:T(8,128)(2,1)} %bitcast.36), calls=%async_computation.1 | async-start | bytes 524288 | tf_op jit(solution)/shard_map/all_to_all | solution.py:159
  96.5 0.7 copy.39
  97.2 14.2 %all_gather.29 = bf16[512,384]{0,1:T(8,128)(2,1)S(1)} all-gather(bf16[128,384]{0,1:T(8,128)(2,1)S(1)} %bitcast.134), channel_id=1, replica_groups=mesh['groups'=2,'seq'=4,'fsdp'=4] {'seq'}, dimensions={0}, use_global_device_ids=true | all-gather | bytes 491520 | tf_op jit(solution)/shard_map/all_gather | solution.py:163
  111.4 0.1 copy.38
  111.6 0.3 fusion.11
  111.8 0.9 copy.40
  112.7 0.5 reduce-scatter.2.cloned.1.call-done
  113.2 1.5 %convert_element_type.44 = bf16[128,256]{1,0:T(8,128)(2,1)} convert(f32[128,256]{1,0:T(8,128)} %reduce-scatter.2.cloned.1.call-done) | non-fusion elementwise | flops 32768 | bytes 196608 | tf_op jit(solution)/shard_map/convert_element_type | solution.py:155
  (21 shorter events, 0.4 us)
Async XLA Ops:
  7.2 106.1 %reduce-scatter.2.cloned.1.call-start = ((), (), s32[]{:S(2)}) async-start(), calls=%async_computation.2 | async-start | bytes 655360 | tf_op jit(solution)/shard_map/reduce_scatter | solution.py:155
  7.2 0.7 copy-start.3
  7.9 0.7 copy-start.2
  9.5 21.6 %copy-start = (bf16[128,1024]{1,0:T(8,128)(2,1)S(1)}, bf16[128,1024]{1,0:T(8,128)(2,1)}, u32[]{:S(2)}) copy-start(bf16[128,1024]{1,0:T(8,128)(2,1)} %param.5) | copy-start | bytes 786436
  45.1 0.8 copy-start.1
  93.0 18.4 %all-to-all-start = ((bf16[128,4,256]{0,2,1:T(8,128)(2,1)}), bf16[128,4,256]{0,2,1:T(8,128)(2,1)S(1)}, u32[]{:S(2)}, u32[]{:S(2)}) async-start(bf16[128,4,256]{0,2,1:T(8,128)(2,1)} %bitcast.36), calls=%async_computation.1 | async-start | bytes 524288 | tf_op jit(solution)/shard_map/all_to_all | solution.py:159
Sparse Core Ops, SparseCore 0:
  92.3 20.8 reduce-scatter.1
where the time goes:
time: 122 us
  blocking collectives  90.5 us (74%)
  between operations  14.2 us (12%)
  matrix products  5.87 us (5%)
  local copies, waits for them, and re-layouts  5.24 us (4%)
  starting transfers between devices  3.44 us (3%)
  other arithmetic  1.84 us (2%)
    all_gather x1, blocking collectives, per_device(): lax.all_gather(qkv_weight, 'seq', axis=0, tiled=True)  21.6 us
    all_gather x1, blocking collectives, per_device(): lax.all_gather(grad_qkv, 'seq', axis=0, tiled=True)  14.2 us
    all_gather x1, blocking collectives, per_device(): far_grads = lax.all_gather(grad_out, 'seq', axis=0, tiled=True)  13.3 us
    all_gather x1, blocking collectives, per_device(): panel = lax.all_gather(key_value, 'seq', axis=0, tiled=True)  12.8 us
    all_gather x1, blocking collectives, per_device(): far_queries = lax.all_gather(query_rows, 'seq', axis=0, tiled=True)  12.3 us
    all_gather x1, blocking collectives, per_device(): lax.all_gather(log_total_rows, 'seq', axis=0, tiled=True)  8.22 us
    all_gather x1, blocking collectives, per_device(): lax.all_gather(grad_dot_rows, 'seq', axis=0, tiled=True)  8.03 us
    unnamed x13, local copies, waits for them, and re-layouts  4.19 us
  transfers between devices with their start and end apart: 2, of which 1 were waited for; matrix products, arithmetic and copies ran while one was open for 2% of the time, Pallas kernels for 0%

commit v1 on v0

--- a/solution.py
+++ b/solution.py
@@ -6,6 +6,28 @@
 HD = 64
 BLOCK = 128
 MASKED_SCORE = -1e30
+
+
+def joined_along(blocks, dim):
+    shape = list(blocks.shape[1:])
+    shape[dim] *= blocks.shape[0]
+    return jnp.moveaxis(blocks, 0, dim).reshape(shape)
+
+
+def grow_blocks(x, axis):
+    size = lax.axis_size(axis)
+    blocks = x[None]
+    for level in range(size.bit_length() - 1):
+        stride = 1 << level
+        other = lax.ppermute(blocks, axis, [(i, i ^ stride) for i in range(size)])
+        both = jnp.stack([blocks, other])
+        upper = lax.axis_index(axis) >> level & 1
+        blocks = jnp.where(upper == 0, both, both[::-1]).reshape(-1, *x.shape)
+    return blocks
+
+
+def doubled_up(x, axis, dim):
+    return joined_along(grow_blocks(x, axis), dim)
 
 
 def query_visible(covisible, block_drive, first_block, block_count):
@@ -41,9 +63,7 @@
     columns_visible = key_visible(covisible, block_drive, first_block, block_count)
     inputs = tokens
     projected = jnp.dot(
-        inputs,
-        lax.all_gather(qkv_weight, "seq", axis=0, tiled=True),
-        preferred_element_type=jnp.float32,
+        inputs, doubled_up(qkv_weight, "seq", 0), preferred_element_type=jnp.float32
     )
     projected = projected.astype(jnp.bfloat16).reshape(local_rows, local_heads, 3, HD)
     queries = projected[:, :, 0, :]

time: 122 us -> 143 us (1.17)
  blocking collectives: 90.5 us -> 108 us
  starting transfers between devices: 3.44 us -> 5.79 us
  matrix products: 5.87 us -> 7.35 us
    all_gather x1, blocking collectives: 13.3 us -> 25.2 us  [per_device(): far_grads = lax.all_gather(grad_out, 'seq', axis=0, tiled=True)]
    all_to_all x0 -> x1, blocking collectives: none -> 9.59 us  [per_device(): lax.all_to_all(tokens, 'seq', split_axis=1, concat_axis=0, tiled=True)]
    ppermute x0 -> x2, starting transfers between devices: none -> 5.75 us  [grow_blocks(): other = lax.ppermute(blocks, axis, [(i, i ^ stride) for i in range(size)])]
    all_gather x1, blocking collectives: 21.6 us -> 17 us  [per_device(): lax.all_gather(qkv_weight, 'seq', axis=0, tiled=True)]
    all_to_all x1 -> x0, starting transfers between devices: 3.41 us -> none  [per_device(): lax.all_to_all(tokens, 'seq', split_axis=1, concat_axis=0, tiled=True)]
    all_gather x1, blocking collectives: 8.03 us -> 9.63 us  [per_device(): lax.all_gather(grad_dot_rows, 'seq', axis=0, tiled=True)]
    unnamed x13 -> x11, local copies, waits for them, and re-layouts: 4.19 us -> 2.81 us
  transfers between devices with their start and end apart: 2 -> 3, of which waited for: 1 -> 0; matrix products, arithmetic and copies ran while one was open for 2% -> 5% of each run, Pallas kernels for 0% -> 0%
where the time goes in v1:
time: 143 us
  blocking collectives  108 us (76%)
  between operations  14.2 us (10%)
  matrix products  7.35 us (5%)
  starting transfers between devices  5.79 us (4%)
  local copies, waits for them, and re-layouts  5.07 us (4%)
  other arithmetic  2.22 us (2%)
    all_gather x1, blocking collectives, per_device(): far_grads = lax.all_gather(grad_out, 'seq', axis=0, tiled=True)  25.2 us
    all_gather x1, blocking collectives, per_device(): lax.all_gather(qkv_weight, 'seq', axis=0, tiled=True)  17 us
    all_gather x1, blocking collectives, per_device(): panel = lax.all_gather(key_value, 'seq', axis=0, tiled=True)  13.5 us
    all_gather x1, blocking collectives, per_device(): lax.all_gather(grad_qkv, 'seq', axis=0, tiled=True)  13.3 us
    all_gather x1, blocking collectives, per_device(): far_queries = lax.all_gather(query_rows, 'seq', axis=0, tiled=True)  12.3 us
    all_gather x1, blocking collectives, per_device(): lax.all_gather(grad_dot_rows, 'seq', axis=0, tiled=True)  9.63 us
    all_to_all x1, blocking collectives, per_device(): lax.all_to_all(tokens, 'seq', split_axis=1, concat_axis=0, tiled=True)  9.59 us
    all_gather x1, blocking collectives, per_device(): lax.all_gather(log_total_rows, 'seq', axis=0, tiled=True)  7.56 us
  transfers between devices with their start and end apart: 3, of which 0 were waited for; matrix products, arithmetic and copies ran while one was open for 5% of the time, Pallas kernels for 0%

profile of v1, /device:TPU:0, one launch (start us, length us, event | category | flops | bytes accessed | tf_op | source)
XLA Modules:
  0.0 142.8 jit_solution(10685395292872830290)
XLA Ops:
  7.2 3.1 %collective-permute-start = (bf16[1,256,384]{2,1,0:T(8,128)(2,1)}, bf16[1,256,384]{2,1,0:T(8,128)(2,1)S(1)}, u32[]{:S(2)}, u32[]{:S(2)}) collective-permute-start(bf16[1,256,384]{2,1,0:T(8,128)(2,1)} %bitcast.150), channel_id=1, source_target_pairs={{0,4},{4,0},{8,12},{12,8},{1,5},{5,1},{9,13},{13,9},{2,6},{6,2},{1... | collective-permute-start | bytes 589832 | tf_op jit(solution)/shard_map/ppermute | solution.py:22
  10.3 1.2 dynamic_slice.11
  11.6 0.8 constant_dynamic-slice_fusion
  12.4 1.6 %fusion.37 = f32[1,512]{1,0:T(1,128)S(1)} fusion(s32[512]{0:T(512)S(1)} %add_select_fusion, s32[4]{0:T(128)} %param.8, s32[4,4]{1,0:T(4,128)} %param.7, s32[]{:T(128)S(6)} %select_n.49, s32[]{:T(128)} %bitcast), kind=kOutput, calls=%fused_computation.52 | convolution fusion | flops 6156 | bytes 5636 | tf_op jit(solution)/shard_map/dot_general | solution.py:76
  14.0 1.6 %fusion.36 = f32[1,512]{1,0:T(1,128)S(1)} fusion(s32[512]{0:T(512)S(1)} %add_select_fusion, s32[4]{0:T(128)} %param.8, s32[4,1]{0,1:T(1,128)S(1)} %copy.45, s32[]{:T(128)} %bitcast), kind=kOutput, calls=%fused_computation.51 | convolution fusion | flops 6156 | bytes 4132 | tf_op jit(solution)/shard_map/dot_general | solution.py:121
  15.7 2.7 %collective-permute-start.1 = (bf16[2,256,384]{2,1,0:T(8,128)(2,1)S(1)}, bf16[2,256,384]{2,1,0:T(8,128)(2,1)S(1)}, u32[]{:S(2)}, u32[]{:S(2)}) collective-permute-start(bf16[2,256,384]{2,1,0:T(8,128)(2,1)S(1)} %get-tuple-element.13), channel_id=1, source_target_pairs={{0,8},{4,12},{8,0},{12,4},{1,9},{5,13},{9,1},{13,5},{2,10},{6,14},... | collective-permute-start | bytes 1179656 | tf_op jit(solution)/shard_map/ppermute | solution.py:22
  18.5 25.2 %all_gather.25 = bf16[512,128]{1,0:T(8,128)(2,1)S(1)} all-gather(bf16[128,128]{1,0:T(8,128)(2,1)S(1)} %copy-done.2), channel_id=1, replica_groups=mesh['groups'=2,'seq'=4,'fsdp'=4] {'seq'}, dimensions={0}, use_global_device_ids=true | all-gather | bytes 163840 | tf_op jit(solution)/shard_map/all_gather | solution.py:118
  43.7 0.1 copy.33
  43.9 17.0 %all_gather.27 = bf16[1024,384]{1,0:T(8,128)(2,1)S(1)} all-gather(bf16[256,384]{1,0:T(8,128)(2,1)S(1)} %copy-done.1), channel_id=1, replica_groups=mesh['groups'=2,'seq'=4,'fsdp'=4] {'seq'}, dimensions={0}, use_global_device_ids=true | all-gather | bytes 983040 | tf_op jit(solution)/shard_map/all_gather | solution.py:171
  61.0 0.1 reverse_select_fusion
  61.2 0.8 copy-done
  61.9 0.4 convolution_convert_fusion
  62.4 13.5 %all_gather.22 = bf16[512,256]{0,1:T(8,128)(2,1)S(1)} all-gather(bf16[128,256]{0,1:T(8,128)(2,1)S(1)} %bitcast.163), channel_id=1, replica_groups=mesh['groups'=2,'seq'=4,'fsdp'=4] {'seq'}, dimensions={0}, use_global_device_ids=true | all-gather | bytes 327680 | tf_op jit(solution)/shard_map/all_gather | solution.py:78
  75.9 0.3 select_reduce_fusion
  76.2 0.2 fusion.24
  76.5 12.3 %all_gather.23 = bf16[512,128]{0,1:T(8,128)(2,1)S(1)} all-gather(bf16[128,128]{0,1:T(8,128)(2,1)S(1)} %bitcast.165), channel_id=1, replica_groups=mesh['groups'=2,'seq'=4,'fsdp'=4] {'seq'}, dimensions={0}, use_global_device_ids=true | all-gather | bytes 163840 | tf_op jit(solution)/shard_map/all_gather | solution.py:117
  88.8 7.6 %all_gather.24 = f32[512,2]{0,1:T(2,128)S(1)} all-gather(f32[128,2]{0,1:T(2,128)S(1)} %bitcast_add_fusion), channel_id=1, replica_groups=mesh['groups'=2,'seq'=4,'fsdp'=4] {'seq'}, dimensions={0}, use_global_device_ids=true | all-gather | bytes 5120 | tf_op jit(solution)/shard_map/all_gather | solution.py:113
  96.3 0.6 multiply_reduce_fusion
  96.9 9.6 %all_gather.26 = f32[512,2]{0,1:T(2,128)S(1)} all-gather(f32[128,2]{0,1:T(2,128)S(1)} %get-tuple-element.16), channel_id=1, replica_groups=mesh['groups'=2,'seq'=4,'fsdp'=4] {'seq'}, dimensions={0}, use_global_device_ids=true | all-gather | bytes 5120 | tf_op jit(solution)/shard_map/all_gather | solution.py:114
  106.5 0.4 fusion.6
  106.9 0.2 fusion.20
  107.1 0.4 fusion.19
  107.5 0.5 fusion.18
  108.0 1.2 fusion.64
  109.2 0.2 copy.36
  109.4 9.6 %all_to_all.19 = bf16[128,4,256]{0,2,1:T(8,128)(2,1)S(1)} all-to-all(bf16[128,4,256]{0,2,1:T(8,128)(2,1)S(1)} %bitcast.146), channel_id=1, replica_groups=mesh['groups'=2,'seq'=4,'fsdp'=4] {'seq'}, dimensions={1} | all-to-all | bytes 524288 | tf_op jit(solution)/shard_map/all_to_all | solution.py:179
  119.0 0.1 copy.37
  119.2 0.7 copy.38
  119.9 13.3 %all_gather.28 = bf16[512,384]{0,1:T(8,128)(2,1)S(1)} all-gather(bf16[128,384]{0,1:T(8,128)(2,1)S(1)} %bitcast.149), channel_id=1, replica_groups=mesh['groups'=2,'seq'=4,'fsdp'=4] {'seq'}, dimensions={0}, use_global_device_ids=true | all-gather | bytes 491520 | tf_op jit(solution)/shard_map/all_gather | solution.py:183
  133.2 0.3 fusion.11
  133.4 0.9 copy.39
  134.4 1.5 %convert_element_type.48 = bf16[128,256]{1,0:T(8,128)(2,1)} convert(f32[128,256]{1,0:T(8,128)} %reduce-scatter.2.cloned.1.call-done) | non-fusion elementwise | flops 32768 | bytes 196608 | tf_op jit(solution)/shard_map/convert_element_type | solution.py:175
  (25 shorter events, 0.6 us)
Async XLA Ops:
  7.2 8.4 %copy-start.1 = (bf16[256,384]{1,0:T(8,128)(2,1)S(1)}, bf16[256,384]{1,0:T(8,128)(2,1)}, u32[]{:S(2)}) copy-start(bf16[256,384]{1,0:T(8,128)(2,1)} %param.6) | copy-start | bytes 589828
  7.2 127.2 %reduce-scatter.2.cloned.1.call-start = ((), (), s32[]{:S(2)}) async-start(), calls=%async_computation.2 | async-start | bytes 655360 | tf_op jit(solution)/shard_map/reduce_scatter | solution.py:175
  7.2 8.3 %collective-permute-start = (bf16[1,256,384]{2,1,0:T(8,128)(2,1)}, bf16[1,256,384]{2,1,0:T(8,128)(2,1)S(1)}, u32[]{:S(2)}, u32[]{:S(2)}) collective-permute-start(bf16[1,256,384]{2,1,0:T(8,128)(2,1)} %bitcast.150), channel_id=1, source_target_pairs={{0,4},{4,0},{8,12},{12,8},{1,5},{5,1},{9,13},{13,9},{2,6},{6,2},{1... | collective-permute-start | bytes 589832 | tf_op jit(solution)/shard_map/ppermute | solution.py:22
  15.6 2.8 %copy-start.2 = (bf16[128,128]{1,0:T(8,128)(2,1)S(1)}, bf16[128,128]{1,0:T(8,128)(2,1)}, u32[]{:S(2)}) copy-start(bf16[128,128]{1,0:T(8,128)(2,1)} %param.9) | copy-start | bytes 98308
  15.7 45.1 %collective-permute-start.1 = (bf16[2,256,384]{2,1,0:T(8,128)(2,1)S(1)}, bf16[2,256,384]{2,1,0:T(8,128)(2,1)S(1)}, u32[]{:S(2)}, u32[]{:S(2)}) collective-permute-start(bf16[2,256,384]{2,1,0:T(8,128)(2,1)S(1)} %get-tuple-element.13), channel_id=1, source_target_pairs={{0,8},{4,12},{8,0},{12,4},{1,9},{5,13},{9,1},{13,5},{2,10},{6,14},... | collective-permute-start | bytes 1179656 | tf_op jit(solution)/shard_map/ppermute | solution.py:22
  61.0 1.0 copy-start
Sparse Core Ops, SparseCore 0:
  109.4 19.8 reduce-scatter.1
